TPU v7x, 128 devices: a whole 4x4x4 slice. The times are simulated.
128 devices in a mesh: gx: 4 (over y), gy: 8 (over z_lo, x), gz: 4 (over z_hi, core).
Axes of the slice: x: 4, y: 4, z: 4 (z_hi: 2, z_lo: 2; z = z_hi * 2 + z_lo), core: 2. Of those that a mesh axis runs over, the one named last changes fastest.
Arguments:
- solution: float32 [16, 64, 128, 512], P(None, 'gx', 'gy', 'gz'), may hold values from -6 to 6
- residual: float32 [16, 64, 128, 512], P(None, 'gx', 'gy', 'gz'), may hold values from -15 to 15, as said below
- direction: float32 [16, 64, 128, 512], P(None, 'gx', 'gy', 'gz'), may hold values from -13 to 13, as said below
- kappa_squared: float32 [64, 128, 512], P('gx', 'gy', 'gz'), may hold values from 0.02 to 0.2
- conductance: float32 [64, 128, 512], P('gx', 'gy', 'gz'), may hold values from 0.1 to 1
Outputs:
- new_solution: float32 [16, 64, 128, 512], P(None, 'gx', 'gy', 'gz')
- new_residual: float32 [16, 64, 128, 512], P(None, 'gx', 'gy', 'gz')
- new_direction: float32 [16, 64, 128, 512], P(None, 'gx', 'gy', 'gz')
Inputs may be any that keep to these rules, and one draw needn't show every extreme that they name: residual is drawn with a part that is independent for each sample and each cell. direction is correlated with residual, sample by sample.
All inputs are finite; a program needn't handle non-finite values.
Results may differ from a plain program's by a relative error of at most 0.0003.
Values sent between devices are 32-bit elements; how exact they have to be, the bound alone decides.
No kernel may reach another device: no remote copies, remote signals or barrier semaphores. Data moves between devices by JAX's collectives and lax.ppermute only.
A program may use at most 128 MiB of HBM per device.

v0:
```python
import jax
import jax.numpy as jnp
from jax import lax
from jax.sharding import PartitionSpec as P

ITERS = 2


def with_halo(block, sides, width):
    for axis, dim in sides:
        count = lax.axis_size(axis)
        forward = [(i, i + 1) for i in range(count - 1)]
        backward = [(target, source) for source, target in forward]
        low = lax.ppermute(
            lax.slice_in_dim(block, block.shape[dim] - width, None, axis=dim), axis, forward
        )
        high = lax.ppermute(lax.slice_in_dim(block, 0, width, axis=dim), axis, backward)
        block = jnp.concatenate([low, block, high], axis=dim)
    return block


def six_sides(array):
    return [
        array[..., 2:, 1:-1, 1:-1],
        array[..., :-2, 1:-1, 1:-1],
        array[..., 1:-1, 2:, 1:-1],
        array[..., 1:-1, :-2, 1:-1],
        array[..., 1:-1, 1:-1, 2:],
        array[..., 1:-1, 1:-1, :-2],
    ]


def laplace(padded, kappa, conduct):
    centre = padded[..., 1:-1, 1:-1, 1:-1]
    conduct_mid = conduct[1:-1, 1:-1, 1:-1]
    total = kappa * centre
    for beside, face_dif in zip(six_sides(padded), six_sides(conduct)):
        total = total + 0.5 * (conduct_mid + face_dif) * (centre - beside)
    return total


def local_gram(first, second, count):
    return (
        jnp.dot(
            first.reshape(first.shape[0], -1),
            second.reshape(second.shape[0], -1).T,
            precision=lax.Precision.HIGHEST,
        )
        / count
    )


def symmetric(matrix):
    return 0.5 * (matrix + matrix.T)


def spd_solve(matrix, right):
    factor = jnp.linalg.cholesky(matrix)
    inner = lax.linalg.triangular_solve(factor, right, left_side=True, lower=True)
    return lax.linalg.triangular_solve(factor, inner, left_side=True, lower=True, transpose_a=True)


def combine(matrix, fields):
    flat = fields.reshape(fields.shape[0], -1)
    return jnp.dot(matrix, flat, precision=lax.Precision.HIGHEST).reshape(fields.shape)


def single_pass(field, kappa, conduct):
    padded = with_halo(field, (("gx", 1), ("gy", 2), ("gz", 3)), 1)
    return laplace(padded, kappa, conduct)


def body(solution, residual, direction, kappa_squared, conductance):
    samples, cells_x, cells_y, cells_z = direction.shape
    devices_all = lax.axis_size("gx") * lax.axis_size("gy") * lax.axis_size("gz")
    count = jnp.float32(cells_x * cells_y * cells_z * devices_all)
    coefs = with_halo(jnp.stack([kappa_squared, conductance]), (("gx", 1), ("gy", 2), ("gz", 3)), 2)
    kappa_mid = coefs[0, 2:-2, 2:-2, 2:-2]
    conduct_one = coefs[1, 1:-1, 1:-1, 1:-1]
    identity = jnp.eye(samples, dtype=jnp.float32)
    for iteration in range(ITERS):
        middle = single_pass(direction, kappa_mid, conduct_one)
        image = single_pass(middle, kappa_mid, conduct_one)
        dir_img, dir_res = lax.psum(
            (local_gram(direction, image, count), local_gram(direction, residual, count)),
            ("gx", "gy", "gz"),
        )
        curvature = symmetric(dir_img)
        step_mat = spd_solve(curvature, dir_res)
        solution = solution + combine(step_mat.T, direction)
        residual = residual - combine(step_mat.T, image)
        img_new = lax.psum(local_gram(image, residual, count), ("gx", "gy", "gz"))
        correction = -spd_solve(curvature, img_new)
        fresh = residual + combine(correction.T, direction)
        norms_mat = lax.psum(local_gram(fresh, fresh, count), ("gx", "gy", "gz"))
        factor = jnp.linalg.cholesky(symmetric(norms_mat))
        inverse = lax.linalg.triangular_solve(factor, identity, left_side=True, lower=True)
        direction = combine(inverse, fresh)
    return (solution, residual, direction)


def solution(mesh):
    in_specs = (
        P(None, "gx", "gy", "gz"),
        P(None, "gx", "gy", "gz"),
        P(None, "gx", "gy", "gz"),
        P("gx", "gy", "gz"),
        P("gx", "gy", "gz"),
    )
    out_specs = (P(None, "gx", "gy", "gz"), P(None, "gx", "gy", "gz"), P(None, "gx", "gy", "gz"))
    return jax.shard_map(body, mesh=mesh, in_specs=in_specs, out_specs=out_specs, check_vma=False)
```

profile of v0, /device:TPU:1, one launch (start us, length us, event | category | flops | bytes accessed | tf_op | source)
XLA Modules:
  0.0 767.0 jit_solution(1931507717396356238)
XLA Ops:
  27.1 4.6 collective-permute-start.9
  32.0 9.8 %collective-permute-start.4 = (f32[2,20,20,2]{3,2,1,0:T(8,128)S(1)}, f32[2,20,20,2]{3,2,1,0:T(8,128)S(1)}, u32[]{:S(2)}, u32[]{:S(2)}) collective-permute-start(f32[2,20,20,2]{3,2,1,0:T(8,128)S(1)} %get-tuple-element.58), channel_id=1, source_target_pairs={{0,1},{1,2},{2,3},{4,5},{5,6},{6,7},{8,9},{9,10},{10,11},{12,13},{... | collective-permute-start | bytes 19208 | tf_op jit(solution)/shard_map/ppermute | solution.py:14
  43.7 4.8 collective-permute-done.4
  48.5 4.9 collective-permute-done.5
  69.7 5.1 collective-permute-start.11
  79.1 4.1 copy.549
  83.2 8.6 %fusion.64 = f32[16,16,16,128]{3,2,1,0:T(8,128)S(1)} fusion(f32[16,16,16,128]{3,2,1,0:T(8,128)S(1)} %copy-done, f32[16,18,18,1]{3,2,1,0:T(8,128)} %copy.549, f32[16,18,1,128]{3,2,1,0:T(1,128)S(1)} %copy-done.20, f32[16,18,16,128]{3,2,1,0:T(8,128)} %copy-done.13, f32[16,18,1,128]{3,2,1,0:T(1,128)S(1)} %copy-done.22, f32[16,18,18,1]{3,2,1,0:T(8,128)} %copy.547, ...), kind=kLoop, calls=%fused_computation.119 | loop fusion | flops 15204352 | bytes 8069632 | tf_op jit(solution)/shard_map/add | solution.py:38
  100.7 4.3 collective-permute-start.15
  123.1 5.1 collective-permute-start.17
  128.3 6.3 fusion.139
  137.5 4.2 copy.557
  141.7 4.1 copy.559
  145.7 12.2 %fusion.46 = f32[16,16,16,128]{3,2,1,0:T(8,128)S(1)} fusion(f32[16,16,16,128]{3,2,1,0:T(8,128)} %copy-done.4, f32[16,18,18,1]{3,2,1,0:T(8,128)} %copy.559, f32[16,18,1,128]{3,2,1,0:T(1,128)S(1)} %copy.551, f32[16,18,1,128]{3,2,1,0:T(1,128)S(1)} %copy.553, f32[16,1,16,128]{3,2,1,0:T(8,128)S(1)} %collective-permute-done.12, f32[16,1,16,128]{3,2,1,0:T(8,128)} %copy-done.24, ...), kind=kLoop, calls=%fused_computation.83 | loop fusion | flops 19398656 | bytes 5710336 | tf_op jit(solution)/shard_map/add | solution.py:38
  157.9 4.8 fusion.149
  165.7 72.3 %all-reduce.1 = (f32[16,16]{1,0:T(8,128)S(1)}, f32[16,16]{0,1:T(8,128)S(1)}) all-reduce(f32[16,16]{1,0:T(8,128)S(1)} %fusion.139, f32[16,16]{0,1:T(8,128)S(1)} %fusion.149), channel_id=1, replica_groups=mesh['gx'=4,'gy'=8,'gz'=4] {'gx','gy','gz'}, use_global_device_ids=true, to_apply=%region_3.0 | all-reduce | flops 512 | bytes 4096 | tf_op jit(solution)/shard_map/psum | solution.py:84
  242.5 6.2 copy_subtract_fusion
  252.3 63.0 %psum.58 = f32[16,16]{1,0:T(8,128)S(1)} all-reduce(f32[16,16]{1,0:T(8,128)S(1)} %fusion.154), channel_id=1, replica_groups=mesh['gx'=4,'gy'=8,'gz'=4] {'gx','gy','gz'}, use_global_device_ids=true, to_apply=%region_4.8 | all-reduce | flops 256 | bytes 2048 | tf_op jit(solution)/shard_map/psum | solution.py:92
  315.7 4.4 fusion.103
  325.1 64.1 %psum.59 = f32[16,16]{1,0:T(8,128)S(1)} all-reduce(f32[16,16]{1,0:T(8,128)S(1)} %fusion.134), channel_id=1, replica_groups=mesh['gx'=4,'gy'=8,'gz'=4] {'gx','gy','gz'}, use_global_device_ids=true, to_apply=%region_5.9 | all-reduce | flops 256 | bytes 2048 | tf_op jit(solution)/shard_map/psum | solution.py:95
  393.5 4.4 fusion.5
  422.5 5.1 collective-permute-start.22
  438.7 4.1 copy.589
  442.8 9.5 %fusion.28 = f32[16,16,16,128]{3,2,1,0:T(8,128)S(1)} fusion(f32[16,16,16,128]{3,2,1,0:T(8,128)} %bitcast.244, f32[16,18,18,1]{3,2,1,0:T(8,128)} %copy.589, f32[16,18,1,128]{3,2,1,0:T(1,128)S(1)} %copy.581, f32[16,18,16,128]{3,2,1,0:T(8,128)} %copy-done.14, f32[16,18,1,128]{3,2,1,0:T(1,128)S(1)} %copy.583, f32[16,18,18,1]{3,2,1,0:T(8,128)} %copy.587, ...), kind=kLoop, calls=%fused_computation.55 | loop fusion | flops 15204352 | bytes 8069632 | tf_op jit(solution)/shard_map/add | solution.py:38
  462.0 4.7 collective-permute-start.27
  489.4 5.0 fusion.130
  498.5 4.1 copy.599
  502.5 11.4 %fusion.10 = f32[16,16,16,128]{3,2,1,0:T(8,128)S(1)} fusion(f32[16,16,16,128]{3,2,1,0:T(8,128)} %copy-done.3, f32[16,18,18,1]{3,2,1,0:T(8,128)} %copy.599, f32[16,18,1,128]{3,2,1,0:T(1,128)S(1)} %copy.591, f32[16,18,1,128]{3,2,1,0:T(1,128)S(1)} %copy.593, f32[16,1,16,128]{3,2,1,0:T(8,128)S(1)} %collective-permute-done.24, f32[16,1,16,128]{3,2,1,0:T(8,128)} %copy-done.23, ...), kind=kLoop, calls=%fused_computation.19 | loop fusion | flops 19398656 | bytes 5710336 | tf_op jit(solution)/shard_map/add | solution.py:38
  520.5 70.3 %all-reduce = (f32[16,16]{1,0:T(8,128)S(1)}, f32[16,16]{1,0:T(8,128)S(1)}) all-reduce(f32[16,16]{1,0:T(8,128)S(1)} %fusion.130, f32[16,16]{1,0:T(8,128)S(1)} %fusion.127), channel_id=1, replica_groups=mesh['gx'=4,'gy'=8,'gz'=4] {'gx','gy','gz'}, use_global_device_ids=true, to_apply=%region_7.11 | all-reduce | flops 512 | bytes 4096 | tf_op jit(solution)/shard_map/psum | solution.py:84
  595.5 5.2 fusion.108
  605.6 64.2 %psum.62 = f32[16,16]{1,0:T(8,128)S(1)} all-reduce(f32[16,16]{1,0:T(8,128)S(1)} %fusion.136), channel_id=1, replica_groups=mesh['gx'=4,'gy'=8,'gz'=4] {'gx','gy','gz'}, use_global_device_ids=true, to_apply=%region_8.12 | all-reduce | flops 256 | bytes 2048 | tf_op jit(solution)/shard_map/psum | solution.py:92
  685.2 63.0 %psum.63 = f32[16,16]{1,0:T(8,128)S(1)} all-reduce(f32[16,16]{1,0:T(8,128)S(1)} %fusion.133), channel_id=1, replica_groups=mesh['gx'=4,'gy'=8,'gz'=4] {'gx','gy','gz'}, use_global_device_ids=true, to_apply=%region_9.13 | all-reduce | flops 256 | bytes 2048 | tf_op jit(solution)/shard_map/psum | solution.py:95
  759.6 5.0 copy_add_fusion.1
  (239 shorter events, 216.2 us)
Async XLA Ops:
  1.6 5.3 collective-permute-start
  5.6 4.7 collective-permute-start.1
  11.2 9.9 %collective-permute-start.2 = (f32[2,20,2,128]{3,2,1,0:T(2,128)S(1)}, f32[2,20,2,128]{3,2,1,0:T(2,128)S(1)}, u32[]{:S(2)}, u32[]{:S(2)}) collective-permute-start(f32[2,20,2,128]{3,2,1,0:T(2,128)S(1)} %get-tuple-element.66), channel_id=1, source_target_pairs={{0,4},{4,8},{8,12},{12,16},{16,20},{20,24},{24,28},{1,5},{5,9},{9,... | collective-permute-start | bytes 122888 | tf_op jit(solution)/shard_map/ppermute | solution.py:14
  14.3 6.8 collective-permute-start.3
  16.6 5.6 collective-permute-start.7
  19.9 5.7 collective-permute-start.6
  22.9 30.5 %copy-start.17 = (f32[16,16,128]{2,1,0:T(8,128)S(1)}, f32[16,16,128]{2,1,0:T(8,128)}, u32[]{:S(2)}) copy-start(f32[16,16,128]{2,1,0:T(8,128)} %param.14) | copy-start | bytes 393220
  25.8 28.0 %collective-permute-start.8 = (f32[16,18,1,128]{3,0,2,1:T(8,128)S(1)}, f32[16,18,1,128]{3,0,2,1:T(8,128)S(1)}, u32[]{:S(2)}, u32[]{:S(2)}) collective-permute-start(f32[16,18,1,128]{3,0,2,1:T(8,128)S(1)} %copy.630), channel_id=1, source_target_pairs={{4,0},{8,4},{12,8},{16,12},{20,16},{24,20},{28,24},{5,1},{9,5},{13... | collective-permute-start | bytes 442376 | tf_op jit(solution)/shard_map/ppermute | solution.py:17
  27.1 26.8 %collective-permute-start.9 = (f32[16,18,1,128]{3,0,2,1:T(8,128)S(1)}, f32[16,18,1,128]{3,0,2,1:T(8,128)S(1)}, u32[]{:S(2)}, u32[]{:S(2)}) collective-permute-start(f32[16,18,1,128]{3,0,2,1:T(8,128)S(1)} %copy.631), channel_id=1, source_target_pairs={{0,4},{4,8},{8,12},{12,16},{16,20},{20,24},{24,28},{1,5},{5,9},{9,... | collective-permute-start | bytes 442376 | tf_op jit(solution)/shard_map/ppermute | solution.py:14
  32.0 16.5 %collective-permute-start.4 = (f32[2,20,20,2]{3,2,1,0:T(8,128)S(1)}, f32[2,20,20,2]{3,2,1,0:T(8,128)S(1)}, u32[]{:S(2)}, u32[]{:S(2)}) collective-permute-start(f32[2,20,20,2]{3,2,1,0:T(8,128)S(1)} %get-tuple-element.58), channel_id=1, source_target_pairs={{0,1},{1,2},{2,3},{4,5},{5,6},{6,7},{8,9},{9,10},{10,11},{12,13},{... | collective-permute-start | bytes 19208 | tf_op jit(solution)/shard_map/ppermute | solution.py:14
  41.7 11.7 %collective-permute-start.5 = (f32[2,20,20,2]{3,2,1,0:T(8,128)S(1)}, f32[2,20,20,2]{3,2,1,0:T(8,128)S(1)}, u32[]{:S(2)}, u32[]{:S(2)}) collective-permute-start(f32[2,20,20,2]{3,2,1,0:T(8,128)S(1)} %get-tuple-element.59), channel_id=1, source_target_pairs={{1,0},{2,1},{3,2},{5,4},{6,5},{7,6},{9,8},{10,9},{11,10},{13,12},{... | collective-permute-start | bytes 19208 | tf_op jit(solution)/shard_map/ppermute | solution.py:17
  63.8 11.3 %collective-permute-start.10 = (f32[16,18,18,1]{2,0,3,1:T(8,128)}, f32[16,18,18,1]{2,0,3,1:T(8,128)}, u32[]{:S(2)}, u32[]{:S(2)}) collective-permute-start(f32[16,18,18,1]{2,0,3,1:T(8,128)} %copy.546), channel_id=1, source_target_pairs={{1,0},{2,1},{3,2},{5,4},{6,5},{7,6},{9,8},{10,9},{11,10},{13,12},{... | collective-permute-start | bytes 62216 | tf_op jit(solution)/shard_map/ppermute | solution.py:17
  69.7 9.4 %collective-permute-start.11 = (f32[16,18,18,1]{2,0,3,1:T(8,128)}, f32[16,18,18,1]{2,0,3,1:T(8,128)}, u32[]{:S(2)}, u32[]{:S(2)}) collective-permute-start(f32[16,18,18,1]{2,0,3,1:T(8,128)} %copy.548), channel_id=1, source_target_pairs={{0,1},{1,2},{2,3},{4,5},{5,6},{6,7},{8,9},{9,10},{10,11},{12,13},{... | collective-permute-start | bytes 62216 | tf_op jit(solution)/shard_map/ppermute | solution.py:14
  91.8 5.7 collective-permute-start.12
  93.1 6.0 collective-permute-start.13
  99.3 7.0 collective-permute-start.14
  100.7 7.4 collective-permute-start.15
  116.8 20.8 %collective-permute-start.16 = (f32[16,18,18,1]{2,0,3,1:T(8,128)}, f32[16,18,18,1]{2,0,3,1:T(8,128)}, u32[]{:S(2)}, u32[]{:S(2)}) collective-permute-start(f32[16,18,18,1]{2,0,3,1:T(8,128)} %copy.556), channel_id=1, source_target_pairs={{1,0},{2,1},{3,2},{5,4},{6,5},{7,6},{9,8},{10,9},{11,10},{13,12},{... | collective-permute-start | bytes 62216 | tf_op jit(solution)/shard_map/ppermute | solution.py:17
  123.1 18.5 %collective-permute-start.17 = (f32[16,18,18,1]{2,0,3,1:T(8,128)}, f32[16,18,18,1]{2,0,3,1:T(8,128)}, u32[]{:S(2)}, u32[]{:S(2)}) collective-permute-start(f32[16,18,18,1]{2,0,3,1:T(8,128)} %copy.558), channel_id=1, source_target_pairs={{0,1},{1,2},{2,3},{4,5},{5,6},{6,7},{8,9},{9,10},{10,11},{12,13},{... | collective-permute-start | bytes 62216 | tf_op jit(solution)/shard_map/ppermute | solution.py:14
  248.7 67.0 %copy-start.1 = (f32[16,16,16,128]{3,0,2,1:T(8,128)}, f32[16,16,16,128]{3,0,2,1:T(8,128)S(1)}, u32[]{:S(2)}) copy-start(f32[16,16,16,128]{3,0,2,1:T(8,128)S(1)} %copy_subtract_fusion) | copy-start | bytes 6291460
  398.3 3.2 collective-permute-start.19
  399.6 5.9 collective-permute-start.18
  406.4 5.9 collective-permute-start.20
  407.9 5.9 collective-permute-start.21
  422.5 12.2 %collective-permute-start.22 = (f32[16,18,18,1]{2,0,3,1:T(8,128)}, f32[16,18,18,1]{2,0,3,1:T(8,128)}, u32[]{:S(2)}, u32[]{:S(2)}) collective-permute-start(f32[16,18,18,1]{2,0,3,1:T(8,128)} %copy.586), channel_id=1, source_target_pairs={{1,0},{2,1},{3,2},{5,4},{6,5},{7,6},{9,8},{10,9},{11,10},{13,12},{... | collective-permute-start | bytes 62216 | tf_op jit(solution)/shard_map/ppermute | solution.py:17
  431.6 7.1 collective-permute-start.23
  452.3 7.2 collective-permute-start.24
  453.9 6.6 collective-permute-start.25
  460.7 8.0 %collective-permute-start.26 = (f32[16,18,1,128]{3,0,2,1:T(8,128)S(1)}, f32[16,18,1,128]{3,0,2,1:T(8,128)S(1)}, u32[]{:S(2)}, u32[]{:S(2)}) collective-permute-start(f32[16,18,1,128]{3,0,2,1:T(8,128)S(1)} %copy.590), channel_id=1, source_target_pairs={{4,0},{8,4},{12,8},{16,12},{20,16},{24,20},{28,24},{5,1},{9,5},{13... | collective-permute-start | bytes 442376 | tf_op jit(solution)/shard_map/ppermute | solution.py:17
  462.0 6.9 collective-permute-start.27
  477.6 16.9 %collective-permute-start.28 = (f32[16,18,18,1]{2,0,3,1:T(8,128)}, f32[16,18,18,1]{2,0,3,1:T(8,128)}, u32[]{:S(2)}, u32[]{:S(2)}) collective-permute-start(f32[16,18,18,1]{2,0,3,1:T(8,128)} %copy.596), channel_id=1, source_target_pairs={{1,0},{2,1},{3,2},{5,4},{6,5},{7,6},{9,8},{10,9},{11,10},{13,12},{... | collective-permute-start | bytes 62216 | tf_op jit(solution)/shard_map/ppermute | solution.py:17
  485.4 13.1 %collective-permute-start.29 = (f32[16,18,18,1]{2,0,3,1:T(8,128)}, f32[16,18,18,1]{2,0,3,1:T(8,128)}, u32[]{:S(2)}, u32[]{:S(2)}) collective-permute-start(f32[16,18,18,1]{2,0,3,1:T(8,128)} %copy.598), channel_id=1, source_target_pairs={{0,1},{1,2},{2,3},{4,5},{5,6},{6,7},{8,9},{9,10},{10,11},{12,13},{... | collective-permute-start | bytes 62216 | tf_op jit(solution)/shard_map/ppermute | solution.py:14
  (27 other events, 228.2 us)
where the time goes:
time: 777 us; the launch traced here: 767 us
  blocking collectives  397 us (51%)
  local copies, waits for them, and re-layouts  113 us (15%)
  starting transfers between devices  92.7 us (12%)
  matrix products  67.4 us (9%)
  other arithmetic  65.2 us (8%)
  waiting for transfers between devices  29.5 us (4%)
    psum x2, blocking collectives, body(): lax.psum((local_gram(direction, image, count), local_gram(direction, resi...  143 us
    psum x2, blocking collectives, body(): img_new = lax.psum(local_gram(image, residual, count), ('gx', 'gy', 'gz'))  127 us
    psum x2, blocking collectives, body(): norms_mat = lax.psum(local_gram(fresh, fresh, count), ('gx', 'gy', 'gz'))  127 us
    ppermute x15, starting transfers between devices, with_halo(): lax.ppermute(lax.slice_in_dim(block, block.shape[dim] - width, None, axis...  64.2 us
    add x4, other arithmetic, laplace(): total = total + 0.5 * (conduct_mid + face_dif) * (centre - beside)  41.7 us
    dot_general x8, matrix products, combine(): jnp.dot(matrix, flat, precision=lax.Precision.HIGHEST).reshape(fields.shape)  33.2 us
    slice x12, local copies, waits for them, and re-layouts, with_halo(): lax.slice_in_dim(block, 0, width, axis=dim)  32.8 us
    dot_general x8, matrix products, local_gram(): jnp.dot(first.reshape(first.shape[0], -1), second.reshape(second.shape[0]...  32.4 us
  transfers between devices with their start and end apart: 30, of which 14 were waited for; matrix products, arithmetic and copies ran while one was open for 7% of the time, Pallas kernels for 0%

commit v1 on v0

--- a/solution.py
+++ b/solution.py
@@ -92,7 +92,9 @@
         img_new = lax.psum(local_gram(image, residual, count), ("gx", "gy", "gz"))
         correction = -spd_solve(curvature, img_new)
         fresh = residual + combine(correction.T, direction)
-        norms_mat = lax.psum(local_gram(fresh, fresh, count), ("gx", "gy", "gz"))
+        norms_mat = jnp.sum(
+            lax.all_gather(local_gram(fresh, fresh, count), ("gx", "gy", "gz")), axis=0
+        )
         factor = jnp.linalg.cholesky(symmetric(norms_mat))
         inverse = lax.linalg.triangular_solve(factor, identity, left_side=True, lower=True)
         direction = combine(inverse, fresh)

time: 777 us -> 997 us (1.28)
  blocking collectives: 397 us -> 618 us
    all_gather x0 -> x2, blocking collectives: none -> 353 us  [body(): lax.all_gather(local_gram(fresh, fresh, count), ('gx', 'gy', 'gz'))]
    psum x2 -> x0, blocking collectives: 127 us -> none  [body(): norms_mat = lax.psum(local_gram(fresh, fresh, count), ('gx', 'gy', 'gz'))]
  transfers between devices with their start and end apart: 30 -> 30, of which waited for: 14 -> 14; matrix products, arithmetic and copies ran while one was open for 7% -> 5% of each run, Pallas kernels for 0% -> 0%
where the time goes in v1:
time: 997 us; the launch traced here: 987 us
  blocking collectives  618 us (62%)
  local copies, waits for them, and re-layouts  113 us (11%)
  starting transfers between devices  91.5 us (9%)
  matrix products  67.5 us (7%)
  other arithmetic  65.5 us (7%)
  waiting for transfers between devices  30.2 us (3%)
    all_gather x2, blocking collectives, body(): lax.all_gather(local_gram(fresh, fresh, count), ('gx', 'gy', 'gz'))  353 us
    psum x2, blocking collectives, body(): lax.psum((local_gram(direction, image, count), local_gram(direction, resi...  138 us
    psum x2, blocking collectives, body(): img_new = lax.psum(local_gram(image, residual, count), ('gx', 'gy', 'gz'))  127 us
    ppermute x15, starting transfers between devices, with_halo(): lax.ppermute(lax.slice_in_dim(block, block.shape[dim] - width, None, axis...  63.7 us
    add x4, other arithmetic, laplace(): total = total + 0.5 * (conduct_mid + face_dif) * (centre - beside)  41.7 us
    dot_general x8, matrix products, combine(): jnp.dot(matrix, flat, precision=lax.Precision.HIGHEST).reshape(fields.shape)  33.2 us
    slice x12, local copies, waits for them, and re-layouts, with_halo(): lax.slice_in_dim(block, 0, width, axis=dim)  32.8 us
    dot_general x8, matrix products, local_gram(): jnp.dot(first.reshape(first.shape[0], -1), second.reshape(second.shape[0]...  32.4 us
  transfers between devices with their start and end apart: 30, of which 14 were waited for; matrix products, arithmetic and copies ran while one was open for 5% of the time, Pallas kernels for 0%

profile of v1, /device:TPU:1, one launch (start us, length us, event | category | flops | bytes accessed | tf_op | source)
XLA Modules:
  0.0 987.3 jit_solution(10976028150490434756)
XLA Ops:
  27.1 4.6 collective-permute-start.9
  32.0 9.8 collective-permute-start.4
  43.7 4.8 collective-permute-done.4
  48.5 4.9 collective-permute-done.5
  69.7 5.1 collective-permute-start.11
  79.1 4.1 copy.528
  83.2 8.6 fusion.64
  100.7 4.3 collective-permute-start.15
  123.1 5.1 collective-permute-start.17
  128.3 6.3 fusion.139
  137.5 4.2 copy.536
  141.7 4.1 copy.538
  145.7 12.2 %fusion.46 = f32[16,16,16,128]{3,2,1,0:T(8,128)S(1)} fusion(f32[16,16,16,128]{3,2,1,0:T(8,128)} %copy-done.4, f32[16,18,18,1]{3,2,1,0:T(8,128)} %copy.538, f32[16,18,1,128]{3,2,1,0:T(1,128)S(1)} %copy.530, f32[16,18,1,128]{3,2,1,0:T(1,128)S(1)} %copy.532, f32[16,1,16,128]{3,2,1,0:T(8,128)S(1)} %collective-permute-done.12, f32[16,1,16,128]{3,2,1,0:T(8,128)} %copy-done.24, ...), kind=kLoop, calls=%fused_computation.83 | loop fusion | flops 19398656 | bytes 5710336 | tf_op jit(solution)/shard_map/add | solution.py:38
  157.9 4.8 fusion.149
  165.7 72.3 %all-reduce.1 = (f32[16,16]{1,0:T(8,128)S(1)}, f32[16,16]{0,1:T(8,128)S(1)}) all-reduce(f32[16,16]{1,0:T(8,128)S(1)} %fusion.139, f32[16,16]{0,1:T(8,128)S(1)} %fusion.149), channel_id=1, replica_groups=mesh['gx'=4,'gy'=8,'gz'=4] {'gx','gy','gz'}, use_global_device_ids=true, to_apply=%region_3.0 | all-reduce | flops 512 | bytes 4096 | tf_op jit(solution)/shard_map/psum | solution.py:84
  242.5 6.2 copy_subtract_fusion
  252.3 63.0 %psum.44 = f32[16,16]{1,0:T(8,128)S(1)} all-reduce(f32[16,16]{1,0:T(8,128)S(1)} %fusion.154), channel_id=1, replica_groups=mesh['gx'=4,'gy'=8,'gz'=4] {'gx','gy','gz'}, use_global_device_ids=true, to_apply=%region_4.8 | all-reduce | flops 256 | bytes 2048 | tf_op jit(solution)/shard_map/psum | solution.py:92
  315.7 4.4 fusion.103
  325.1 176.6 %all-gather = f32[2048,16]{1,0:T(8,128)S(1)} all-gather(f32[16,16]{1,0:T(8,128)S(1)} %fusion.134), channel_id=2, replica_groups=mesh['gx'=4,'gy'=8,'gz'=4] {'gx','gy','gz'}, dimensions={0}, use_global_device_ids=true | all-gather | bytes 132096 | tf_op jit(solution)/shard_map/all_gather | solution.py:96
  506.1 4.4 fusion.5
  536.0 4.1 collective-permute-start.22
  551.1 4.1 copy.566
  555.2 9.5 fusion.28
  574.3 4.1 collective-permute-start.27
  589.3 4.2 collective-permute-start.28
  601.5 5.0 fusion.130
  614.6 11.4 %fusion.10 = f32[16,16,16,128]{3,2,1,0:T(8,128)S(1)} fusion(f32[16,16,16,128]{3,2,1,0:T(8,128)} %copy-done.3, f32[16,18,18,1]{3,2,1,0:T(8,128)} %copy.576, f32[16,18,1,128]{3,2,1,0:T(1,128)S(1)} %copy.568, f32[16,18,1,128]{3,2,1,0:T(1,128)S(1)} %copy.570, f32[16,1,16,128]{3,2,1,0:T(8,128)S(1)} %collective-permute-done.24, f32[16,1,16,128]{3,2,1,0:T(8,128)} %copy-done.23, ...), kind=kLoop, calls=%fused_computation.19 | loop fusion | flops 19398656 | bytes 5710336 | tf_op jit(solution)/shard_map/add | solution.py:38
  632.6 65.8 %all-reduce = (f32[16,16]{1,0:T(8,128)S(1)}, f32[16,16]{1,0:T(8,128)S(1)}) all-reduce(f32[16,16]{1,0:T(8,128)S(1)} %fusion.130, f32[16,16]{1,0:T(8,128)S(1)} %fusion.127), channel_id=1, replica_groups=mesh['gx'=4,'gy'=8,'gz'=4] {'gx','gy','gz'}, use_global_device_ids=true, to_apply=%region_7.11 | all-reduce | flops 512 | bytes 4096 | tf_op jit(solution)/shard_map/psum | solution.py:84
  703.1 5.2 fusion.108
  713.2 63.7 %psum.47 = f32[16,16]{1,0:T(8,128)S(1)} all-reduce(f32[16,16]{1,0:T(8,128)S(1)} %fusion.136), channel_id=1, replica_groups=mesh['gx'=4,'gy'=8,'gz'=4] {'gx','gy','gz'}, use_global_device_ids=true, to_apply=%region_8.12 | all-reduce | flops 256 | bytes 2048 | tf_op jit(solution)/shard_map/psum | solution.py:92
  792.3 176.2 %all-gather.1 = f32[2048,16]{1,0:T(8,128)S(1)} all-gather(f32[16,16]{1,0:T(8,128)S(1)} %fusion.133), channel_id=3, replica_groups=mesh['gx'=4,'gy'=8,'gz'=4] {'gx','gy','gz'}, dimensions={0}, use_global_device_ids=true | all-gather | bytes 132096 | tf_op jit(solution)/shard_map/all_gather | solution.py:96
  980.1 5.0 copy_add_fusion.1
  (238 shorter events, 217.4 us)
Async XLA Ops:
  1.6 5.3 collective-permute-start
  5.6 4.7 collective-permute-start.1
  11.2 9.9 %collective-permute-start.2 = (f32[2,20,2,128]{3,2,1,0:T(2,128)S(1)}, f32[2,20,2,128]{3,2,1,0:T(2,128)S(1)}, u32[]{:S(2)}, u32[]{:S(2)}) collective-permute-start(f32[2,20,2,128]{3,2,1,0:T(2,128)S(1)} %get-tuple-element.66), channel_id=1, source_target_pairs={{0,4},{4,8},{8,12},{12,16},{16,20},{20,24},{24,28},{1,5},{5,9},{9,... | collective-permute-start | bytes 122888 | tf_op jit(solution)/shard_map/ppermute | solution.py:14
  14.3 6.8 collective-permute-start.3
  16.6 5.6 collective-permute-start.7
  19.9 5.7 collective-permute-start.6
  22.9 30.5 %copy-start.17 = (f32[16,16,128]{2,1,0:T(8,128)S(1)}, f32[16,16,128]{2,1,0:T(8,128)}, u32[]{:S(2)}) copy-start(f32[16,16,128]{2,1,0:T(8,128)} %param.14) | copy-start | bytes 393220
  25.8 28.0 %collective-permute-start.8 = (f32[16,18,1,128]{3,0,2,1:T(8,128)S(1)}, f32[16,18,1,128]{3,0,2,1:T(8,128)S(1)}, u32[]{:S(2)}, u32[]{:S(2)}) collective-permute-start(f32[16,18,1,128]{3,0,2,1:T(8,128)S(1)} %copy.606), channel_id=1, source_target_pairs={{4,0},{8,4},{12,8},{16,12},{20,16},{24,20},{28,24},{5,1},{9,5},{13... | collective-permute-start | bytes 442376 | tf_op jit(solution)/shard_map/ppermute | solution.py:17
  27.1 26.8 %collective-permute-start.9 = (f32[16,18,1,128]{3,0,2,1:T(8,128)S(1)}, f32[16,18,1,128]{3,0,2,1:T(8,128)S(1)}, u32[]{:S(2)}, u32[]{:S(2)}) collective-permute-start(f32[16,18,1,128]{3,0,2,1:T(8,128)S(1)} %copy.607), channel_id=1, source_target_pairs={{0,4},{4,8},{8,12},{12,16},{16,20},{20,24},{24,28},{1,5},{5,9},{9,... | collective-permute-start | bytes 442376 | tf_op jit(solution)/shard_map/ppermute | solution.py:14
  32.0 16.5 %collective-permute-start.4 = (f32[2,20,20,2]{3,2,1,0:T(8,128)S(1)}, f32[2,20,20,2]{3,2,1,0:T(8,128)S(1)}, u32[]{:S(2)}, u32[]{:S(2)}) collective-permute-start(f32[2,20,20,2]{3,2,1,0:T(8,128)S(1)} %get-tuple-element.58), channel_id=1, source_target_pairs={{0,1},{1,2},{2,3},{4,5},{5,6},{6,7},{8,9},{9,10},{10,11},{12,13},{... | collective-permute-start | bytes 19208 | tf_op jit(solution)/shard_map/ppermute | solution.py:14
  41.7 11.7 %collective-permute-start.5 = (f32[2,20,20,2]{3,2,1,0:T(8,128)S(1)}, f32[2,20,20,2]{3,2,1,0:T(8,128)S(1)}, u32[]{:S(2)}, u32[]{:S(2)}) collective-permute-start(f32[2,20,20,2]{3,2,1,0:T(8,128)S(1)} %get-tuple-element.59), channel_id=1, source_target_pairs={{1,0},{2,1},{3,2},{5,4},{6,5},{7,6},{9,8},{10,9},{11,10},{13,12},{... | collective-permute-start | bytes 19208 | tf_op jit(solution)/shard_map/ppermute | solution.py:17
  63.8 11.3 %collective-permute-start.10 = (f32[16,18,18,1]{2,0,3,1:T(8,128)}, f32[16,18,18,1]{2,0,3,1:T(8,128)}, u32[]{:S(2)}, u32[]{:S(2)}) collective-permute-start(f32[16,18,18,1]{2,0,3,1:T(8,128)} %copy.525), channel_id=1, source_target_pairs={{1,0},{2,1},{3,2},{5,4},{6,5},{7,6},{9,8},{10,9},{11,10},{13,12},{... | collective-permute-start | bytes 62216 | tf_op jit(solution)/shard_map/ppermute | solution.py:17
  69.7 9.4 collective-permute-start.11
  91.8 5.7 collective-permute-start.12
  93.1 6.0 collective-permute-start.13
  99.3 7.0 collective-permute-start.14
  100.7 7.4 collective-permute-start.15
  116.8 20.8 %collective-permute-start.16 = (f32[16,18,18,1]{2,0,3,1:T(8,128)}, f32[16,18,18,1]{2,0,3,1:T(8,128)}, u32[]{:S(2)}, u32[]{:S(2)}) collective-permute-start(f32[16,18,18,1]{2,0,3,1:T(8,128)} %copy.535), channel_id=1, source_target_pairs={{1,0},{2,1},{3,2},{5,4},{6,5},{7,6},{9,8},{10,9},{11,10},{13,12},{... | collective-permute-start | bytes 62216 | tf_op jit(solution)/shard_map/ppermute | solution.py:17
  123.1 18.5 %collective-permute-start.17 = (f32[16,18,18,1]{2,0,3,1:T(8,128)}, f32[16,18,18,1]{2,0,3,1:T(8,128)}, u32[]{:S(2)}, u32[]{:S(2)}) collective-permute-start(f32[16,18,18,1]{2,0,3,1:T(8,128)} %copy.537), channel_id=1, source_target_pairs={{0,1},{1,2},{2,3},{4,5},{5,6},{6,7},{8,9},{9,10},{10,11},{12,13},{... | collective-permute-start | bytes 62216 | tf_op jit(solution)/shard_map/ppermute | solution.py:14
  248.7 67.0 %copy-start.1 = (f32[16,16,16,128]{3,0,2,1:T(8,128)}, f32[16,16,16,128]{3,0,2,1:T(8,128)S(1)}, u32[]{:S(2)}) copy-start(f32[16,16,16,128]{3,0,2,1:T(8,128)S(1)} %copy_subtract_fusion) | copy-start | bytes 6291460
  510.9 4.2 collective-permute-start.19
  512.3 6.8 collective-permute-start.18
  519.9 6.3 collective-permute-start.20
  521.3 6.1 collective-permute-start.21
  536.0 11.0 %collective-permute-start.22 = (f32[16,18,18,1]{2,0,3,1:T(8,128)}, f32[16,18,18,1]{2,0,3,1:T(8,128)}, u32[]{:S(2)}, u32[]{:S(2)}) collective-permute-start(f32[16,18,18,1]{2,0,3,1:T(8,128)} %copy.563), channel_id=1, source_target_pairs={{1,0},{2,1},{3,2},{5,4},{6,5},{7,6},{9,8},{10,9},{11,10},{13,12},{... | collective-permute-start | bytes 62216 | tf_op jit(solution)/shard_map/ppermute | solution.py:17
  544.1 7.0 collective-permute-start.23
  564.7 7.1 collective-permute-start.24
  566.3 6.5 collective-permute-start.25
  573.0 7.4 collective-permute-start.26
  574.3 6.3 collective-permute-start.27
  589.3 17.2 %collective-permute-start.28 = (f32[16,18,18,1]{2,0,3,1:T(8,128)}, f32[16,18,18,1]{2,0,3,1:T(8,128)}, u32[]{:S(2)}, u32[]{:S(2)}) collective-permute-start(f32[16,18,18,1]{2,0,3,1:T(8,128)} %copy.573), channel_id=1, source_target_pairs={{1,0},{2,1},{3,2},{5,4},{6,5},{7,6},{9,8},{10,9},{11,10},{13,12},{... | collective-permute-start | bytes 62216 | tf_op jit(solution)/shard_map/ppermute | solution.py:17
  597.5 13.1 %collective-permute-start.29 = (f32[16,18,18,1]{2,0,3,1:T(8,128)}, f32[16,18,18,1]{2,0,3,1:T(8,128)}, u32[]{:S(2)}, u32[]{:S(2)}) collective-permute-start(f32[16,18,18,1]{2,0,3,1:T(8,128)} %copy.575), channel_id=1, source_target_pairs={{0,1},{1,2},{2,3},{4,5},{5,6},{6,7},{8,9},{9,10},{10,11},{12,13},{... | collective-permute-start | bytes 62216 | tf_op jit(solution)/shard_map/ppermute | solution.py:14
  (27 other events, 227.3 us)
